TPU v7x, 32 devices: a whole 2x2x4 slice. The times are simulated.
32 devices in a mesh: grp: 4 (over z), sub: 8 (over y, x, core).
Axes of the slice: x: 2, y: 2, z: 4, core: 2. Of those that a mesh axis runs over, the one named last changes fastest.
Arguments:
- stiff_blocks: float32 [8, 128, 4, 128, 128], P('grp', 'sub'), may hold values from -0.25 to 0.25
- block_cols: int32 [8, 128, 4], P('grp', 'sub'), may hold values from 0 to 127, as said below
- live_blocks: int32 [8, 8], P('grp', 'sub'), may hold values from 1 to 16, as said below
- sub_diag: float32 [8, 16384], P('grp', 'sub'), may hold values from 0.05 to 1
- penalty: float32 [8, 1024], P('grp', 'sub'), may hold values from 0.5 to 4
- sub_load: float32 [8, 16384], P('grp', 'sub'), may hold values from -6 to 6
- iface_map: int32 [8, 1024], P('grp', 'sub'), may hold values from 0 to 262143
- global_load: float32 [1024, 256], P(('grp', 'sub')), may hold values from -6 to 6
- global_diag: float32 [1024, 256], P(('grp', 'sub')), may hold values from 0.1 to 1
Outputs:
- global_field: float32 [1024, 256], P(('grp', 'sub'))
- sub_field: float32 [8, 16384], P('grp', 'sub')
Inputs may be any that keep to these rules, and one draw needn't show every extreme that they name: `live_blocks`: every live count is at least 1 and at most 16; the first submodel holds 16 live block rows on index 0 of sub. `block_cols`: among the blocks of one submodel's block rows on one index of sub, at most 8 have their column block among the block rows of any one index of sub; in every submodel some index of sub receives exactly 8 such blocks from every index of sub.
All inputs are finite; a program needn't handle non-finite values.
Results may differ from a plain program's by a relative error of at most 0.0003.
Values sent between devices are 32-bit elements; how exact they have to be, the bound alone decides.
No kernel may reach another device: no remote copies, remote signals or barrier semaphores. Data moves between devices by JAX's collectives and lax.ppermute only.
A program may use at most 64 MiB of HBM per device.

v0:
```python
import jax
import jax.numpy as jnp
from jax import lax
from jax.sharding import PartitionSpec as P

CG_STEPS = 2
COUPLE = 2
CAP = 8
HIGH = lax.Precision.HIGHEST


def with_halo(x, sides, width):
    for axis, dim in sides:
        peers, length = (lax.axis_size(axis), x.shape[dim])
        up = [(i, (i + 1) % peers) for i in range(peers - 1)]
        down = [(j, i) for i, j in up]
        last = lax.slice_in_dim(x, length - width, length, axis=dim)
        first = lax.slice_in_dim(x, 0, width, axis=dim)
        before = lax.ppermute(last, axis, up)
        after = lax.ppermute(first, axis, down)
        x = jnp.concatenate([before, x, after], axis=dim)
    return x


def glob_apply(field, gdiag):
    padded = with_halo(field, ((("grp", "sub"), 0),), 1)
    padded = jnp.pad(padded, ((0, 0), (1, 1)))
    beside = padded[2:, 1:-1] + padded[:-2, 1:-1] + padded[1:-1, 2:] + padded[1:-1, :-2]
    return (4.0 + gdiag) * field - beside


def row_sum(left, right):
    return jnp.sum(left * right, axis=1, keepdims=True)


def body(
    stiff_blocks,
    block_cols,
    live_blocks,
    sub_diag,
    penalty,
    sub_load,
    iface_map,
    global_load,
    global_diag,
):
    slots = stiff_blocks.shape[0]
    block_rows = stiff_blocks.shape[1]
    width = stiff_blocks.shape[3]
    rows_dev = block_rows * width
    gx_rows, gy_cols = global_load.shape
    glob_local = gx_rows * gy_cols
    groups_sub = lax.axis_size("sub")
    me_flat = lax.axis_index("grp") * groups_sub + lax.axis_index("sub")
    blocks = jnp.arange(rows_dev, dtype=jnp.int32) // width
    mask = (blocks[None, :] < live_blocks).astype(jnp.float32)
    pen_full = jnp.concatenate([penalty, jnp.zeros((slots, rows_dev - width), jnp.float32)], axis=1)
    dsum = sub_diag + pen_full
    flat_cols = block_cols.reshape(slots, -1)
    owner_of = flat_cols // block_rows
    local_of = flat_cols % block_rows
    owner_hot = (owner_of[..., None] == jnp.arange(groups_sub, dtype=jnp.int32)).astype(jnp.int32)
    earlier = jnp.cumsum(owner_hot, axis=1) - owner_hot
    rank_of = jnp.sum(earlier * owner_hot, axis=2)
    bucket_of = owner_of * CAP + rank_of
    placing = (bucket_of[..., None] == jnp.arange(groups_sub * CAP, dtype=jnp.int32)).astype(
        jnp.float32
    )
    send_ids = jnp.einsum("sqk,sq->sk", placing, (local_of + 1).astype(jnp.float32), precision=HIGH)
    send_ids = send_ids.reshape(slots, groups_sub, CAP)

    def sub_apply(vector):
        whole = lax.all_gather(vector, "sub", axis=1, tiled=True)
        tiles = whole.reshape(slots, -1, width)
        picked = jax.vmap(lambda table, index: table[index])(tiles, block_cols)
        strain = jnp.einsum("srnij,srnj->sri", stiff_blocks, picked, precision=HIGH)
        terms = jnp.einsum("srnij,sri->srnj", stiff_blocks, strain, precision=HIGH)
        targets = jnp.arange(block_rows * lax.axis_size("sub"), dtype=jnp.int32)
        onehot = (block_cols[..., None] == targets).astype(jnp.float32)
        back = lax.psum_scatter(
            jnp.einsum("srnm,srnj->msj", onehot, terms, precision=HIGH),
            "sub",
            scatter_dimension=0,
            tiled=True,
        )
        back = jnp.transpose(back, (1, 0, 2)).reshape(slots, rows_dev)
        return mask * (dsum * vector + back)

    all_map = lax.all_gather(iface_map, ("grp", "sub"), axis=0, tiled=True)
    local_idx = all_map - me_flat * glob_local
    valid = (local_idx >= 0) & (local_idx < glob_local)
    seg_idx = jnp.where(valid, local_idx, glob_local)
    global_field = jnp.zeros_like(global_load)
    sub_field = jnp.zeros_like(sub_load)
    for outer in range(COUPLE):
        if outer == 0:
            bvals = jnp.zeros_like(penalty)
        else:
            whole_field = lax.all_gather(global_field, ("grp", "sub"), axis=0, tiled=True)
            bvals = whole_field.reshape(-1)[iface_map]
        b_full = jnp.concatenate([bvals, jnp.zeros((slots, rows_dev - width), jnp.float32)], axis=1)
        rhs = mask * (sub_load + pen_full * b_full)
        field = sub_field
        if outer == 0:
            resid = rhs
        else:
            resid = rhs - sub_apply(field)

        def norm_sum(vector):
            return lax.psum(row_sum(vector, vector), "sub")

        direction = resid
        norm_now = norm_sum(resid)
        for step in range(CG_STEPS):
            image = sub_apply(direction)
            alpha = norm_now / lax.psum(row_sum(direction, image), "sub")
            field = field + alpha * direction
            resid = resid - alpha * image
            if step + 1 < CG_STEPS:
                norm_next = norm_sum(resid)
                direction = resid + norm_next / norm_now * direction
                norm_now = norm_next
        sub_field = field
        lam = penalty * (sub_field[:, :width] - bvals)
        lam_all = lax.all_gather(lam, ("grp", "sub"), axis=0, tiled=True)
        lam_g = jax.ops.segment_sum(
            lam_all.reshape(-1), seg_idx.reshape(-1), num_segments=glob_local + 1
        )
        lam_g = lam_g[:glob_local].reshape(gx_rows, gy_cols)
        if outer == 0:
            resid_g = global_load + lam_g
        else:
            resid_g = global_load - glob_apply(global_field, global_diag) + lam_g
        image_g = glob_apply(resid_g, global_diag)
        top, bottom = lax.psum(
            (jnp.sum(resid_g * resid_g), jnp.sum(resid_g * image_g)), ("grp", "sub")
        )
        global_field = global_field + top / bottom * resid_g
    return (global_field, sub_field)


def solution(mesh):
    return jax.shard_map(
        body,
        mesh=mesh,
        in_specs=(
            P("grp", "sub", None, None, None),
            P("grp", "sub", None),
            P("grp", "sub"),
            P("grp", "sub"),
            P("grp", "sub"),
            P("grp", "sub"),
            P("grp", "sub"),
            P(("grp", "sub"), None),
            P(("grp", "sub"), None),
        ),
        out_specs=(P(("grp", "sub"), None), P("grp", "sub")),
        check_vma=False,
    )
```

profile of v0, /device:TPU:12, one launch (start us, length us, event | category | flops | bytes accessed | tf_op | source)
XLA Modules:
  0.0 802.4 jit_solution(16290601400072708618)
XLA Ops:
  8.9 9.2 %all_gather.28 = f32[2,16384]{1,0:T(2,128)S(1)} all-gather(f32[2,2048]{1,0:T(2,128)S(1)} %compare_select_fusion.6), channel_id=1, replica_groups=mesh['grp'=4,'sub'=8] {'sub'}, dimensions={1}, use_global_device_ids=true | all-gather | bytes 147456 | tf_op jit(solution)/shard_map/all_gather | solution.py:73
  19.4 10.1 %convolution_bitcast_fusion.9 = f32[2,16,128,1,1]{2,3,4,1,0:T(1,128)S(1)} fusion(f32[2,16,4,128,1]{3,4,2,1,0:T(1,128)S(1)} %bitcast.242, f32[2,16,4,128,128]{4,3,2,1,0:T(8,128)} %param.9), kind=kOutput, calls=%fused_computation.17 | convolution fusion | flops 25165824 | bytes 8470528 | tf_op jit(solution)/shard_map/srnij,srnj->sri/dot_general | solution.py:76
  34.8 30.8 %all-gather = s32[32,2,128]{2,1,0:T(2,128)S(1)} all-gather(s32[1,2,128]{2,1,0:T(2,128)S(1)} %bitcast.257), channel_id=1, replica_groups=mesh['grp'=4,'sub'=8] {'grp','sub'}, dimensions={0}, use_global_device_ids=true | all-gather | bytes 33792 | tf_op jit(solution)/shard_map/all_gather | solution.py:89
  66.8 20.5 %all-reduce.20.cloned.1.call-done = f32[128,2,128]{2,1,0:T(2,128)} async-done(((f32[128,2,128]{2,1,0:T(2,128)}), f32[128,2,128]{2,1,0:T(2,128)}) %all-reduce.20.cloned.1.call-update) | async-done | bytes 131088
  88.3 11.8 %all-reduce.13 = (f32[2,1]{0,1:T(1,128)S(1)}, f32[2,1]{0,1:T(1,128)S(1)}) all-reduce(f32[2,1]{0,1:T(1,128)S(1)} %bitcast.259, f32[2,1]{0,1:T(1,128)S(1)} %bitcast.258), channel_id=1, replica_groups=mesh['grp'=4,'sub'=8] {'sub'}, use_global_device_ids=true, to_apply=%region_1.2 | all-reduce | flops 4 | bytes 32 | tf_op jit(solution)/shard_map/psum | solution.py:110
  100.3 11.8 %psum.86 = f32[2,1]{0,1:T(1,128)S(1)} all-reduce(f32[2,1]{0,1:T(1,128)S(1)} %bitcast.264), channel_id=1, replica_groups=mesh['grp'=4,'sub'=8] {'sub'}, use_global_device_ids=true, to_apply=%region_6.7 | all-reduce | flops 2 | bytes 16 | tf_op jit(solution)/shard_map/psum | solution.py:110
  112.2 9.3 %all_gather.29 = f32[2,16384]{1,0:T(2,128)S(1)} all-gather(f32[2,2048]{1,0:T(2,128)S(1)} %multiply_add_fusion.4), channel_id=1, replica_groups=mesh['grp'=4,'sub'=8] {'sub'}, dimensions={1}, use_global_device_ids=true | all-gather | bytes 147456 | tf_op jit(solution)/shard_map/all_gather | solution.py:73
  122.8 9.2 %convolution_bitcast_fusion.8 = f32[2,16,128,1,1]{2,3,4,1,0:T(1,128)S(1)} fusion(f32[2,16,4,128,1]{3,4,2,1,0:T(1,128)S(1)} %bitcast.243, f32[2,16,4,128,128]{4,3,2,1,0:T(8,128)} %param.9), kind=kOutput, calls=%fused_computation.16 | convolution fusion | flops 25165824 | bytes 8470528 | tf_op jit(solution)/shard_map/srnij,srnj->sri/dot_general | solution.py:76
  132.0 6.4 fusion.54
  139.6 52.7 %all-reduce.22.cloned.1.call-done = f32[128,2,128]{2,1,0:T(2,128)} async-done(((f32[128,2,128]{2,1,0:T(2,128)}), f32[128,2,128]{2,1,0:T(2,128)}) %all-reduce.22.cloned.1.call-update) | async-done | bytes 131088
  193.2 11.8 %psum.87 = f32[2,1]{0,1:T(1,128)S(1)} all-reduce(f32[2,1]{0,1:T(1,128)S(1)} %bitcast.263), channel_id=1, replica_groups=mesh['grp'=4,'sub'=8] {'sub'}, use_global_device_ids=true, to_apply=%region_9.10 | all-reduce | flops 2 | bytes 16 | tf_op jit(solution)/shard_map/psum | solution.py:116
  205.1 29.1 %all-gather.1 = f32[32,2,128]{2,1,0:T(2,128)S(1)} all-gather(f32[1,2,128]{2,1,0:T(2,128)S(1)} %fusion.49), channel_id=1, replica_groups=mesh['grp'=4,'sub'=8] {'grp','sub'}, dimensions={0}, use_global_device_ids=true | all-gather | bytes 33792 | tf_op jit(solution)/shard_map/all_gather | solution.py:125
  234.2 55.2 %scatter_custom_fusion = f32[8193]{0:T(1024)S(1)} fusion(s32[8192]{0:T(1024)S(1)} %select_bitcast_fusion, f32[8192]{0:T(1024)S(1)} %bitcast.249, f32[]{:T(128)} %constant.41.clone.1), kind=kCustom, calls=%fused_computation.88 | custom fusion | flops 8192 | bytes 32776 | tf_op jit(solution)/shard_map/scatter-add | solution.py:126
  298.9 46.9 %all-reduce.11 = (f32[]{:T(128)}, f32[]{:T(128)}) all-reduce(f32[]{:T(128)} %get-tuple-element.5, f32[]{:T(128)} %get-tuple-element.4), channel_id=1, replica_groups=mesh['grp'=4,'sub'=8] {'grp','sub'}, use_global_device_ids=true, to_apply=%region_12.13 | all-reduce | flops 2 | bytes 16 | tf_op jit(solution)/shard_map/psum | solution.py:135
  347.9 8.8 %all_gather.32 = f32[2,16384]{1,0:T(2,128)S(1)} all-gather(f32[2,2048]{1,0:T(2,128)S(1)} %multiply_add_fusion.3), channel_id=1, replica_groups=mesh['grp'=4,'sub'=8] {'sub'}, dimensions={1}, use_global_device_ids=true | all-gather | bytes 147456 | tf_op jit(solution)/shard_map/all_gather | solution.py:73
  357.9 9.2 %convolution_bitcast_fusion.7 = f32[2,16,128,1,1]{2,3,4,1,0:T(1,128)S(1)} fusion(f32[2,16,4,128,1]{3,4,2,1,0:T(1,128)S(1)} %bitcast.244, f32[2,16,4,128,128]{4,3,2,1,0:T(8,128)} %param.9), kind=kOutput, calls=%fused_computation.15 | convolution fusion | flops 25165824 | bytes 8470528 | tf_op jit(solution)/shard_map/srnij,srnj->sri/dot_general | solution.py:76
  367.1 6.4 fusion.55
  374.6 24.8 %all-gather.5.cloned.1.call-done = f32[1024,256]{1,0:T(8,128)} async-done(((f32[32,256]{1,0:T(8,128)}), f32[1024,256]{1,0:T(8,128)}) %all-gather.5.cloned.1.call-update) | async-done | bytes 1048592 | tf_op jit(solution)/shard_map/all_gather | solution.py:99
  402.9 51.4 %all-reduce.24.cloned.1.call-done = f32[128,2,128]{2,1,0:T(2,128)} async-done(((f32[128,2,128]{2,1,0:T(2,128)}), f32[128,2,128]{2,1,0:T(2,128)}) %all-reduce.24.cloned.1.call-update) | async-done | bytes 131088
  455.2 9.1 %all_gather.33 = f32[2,16384]{1,0:T(2,128)S(1)} all-gather(f32[2,2048]{1,0:T(2,128)S(1)} %fusion.35), channel_id=1, replica_groups=mesh['grp'=4,'sub'=8] {'sub'}, dimensions={1}, use_global_device_ids=true | all-gather | bytes 147456 | tf_op jit(solution)/shard_map/all_gather | solution.py:73
  465.5 9.2 %convolution_bitcast_fusion.6 = f32[2,16,128,1,1]{2,3,4,1,0:T(1,128)S(1)} fusion(f32[2,16,4,128,1]{3,4,2,1,0:T(1,128)S(1)} %bitcast.245, f32[2,16,4,128,128]{4,3,2,1,0:T(8,128)} %param.9), kind=kOutput, calls=%fused_computation.14 | convolution fusion | flops 25165824 | bytes 8470528 | tf_op jit(solution)/shard_map/srnij,srnj->sri/dot_general | solution.py:76
  474.7 6.4 fusion.56
  488.8 46.2 %all-reduce.26.cloned.1.call-done = f32[128,2,128]{2,1,0:T(2,128)} async-done(((f32[128,2,128]{2,1,0:T(2,128)}), f32[128,2,128]{2,1,0:T(2,128)}) %all-reduce.26.cloned.1.call-update) | async-done | bytes 131088
  535.9 11.8 %all-reduce.12 = (f32[2,1]{0,1:T(1,128)S(1)}, f32[2,1]{0,1:T(1,128)S(1)}) all-reduce(f32[2,1]{0,1:T(1,128)S(1)} %bitcast.261, f32[2,1]{0,1:T(1,128)S(1)} %bitcast.260), channel_id=1, replica_groups=mesh['grp'=4,'sub'=8] {'sub'}, use_global_device_ids=true, to_apply=%region_17.18 | all-reduce | flops 4 | bytes 32 | tf_op jit(solution)/shard_map/psum | solution.py:110
  547.9 11.8 %psum.92 = f32[2,1]{0,1:T(1,128)S(1)} all-reduce(f32[2,1]{0,1:T(1,128)S(1)} %bitcast.265), channel_id=1, replica_groups=mesh['grp'=4,'sub'=8] {'sub'}, use_global_device_ids=true, to_apply=%region_22.23 | all-reduce | flops 2 | bytes 16 | tf_op jit(solution)/shard_map/psum | solution.py:110
  559.8 9.1 %all_gather.34 = f32[2,16384]{1,0:T(2,128)S(1)} all-gather(f32[2,2048]{1,0:T(2,128)S(1)} %multiply_add_fusion.2), channel_id=1, replica_groups=mesh['grp'=4,'sub'=8] {'sub'}, dimensions={1}, use_global_device_ids=true | all-gather | bytes 147456 | tf_op jit(solution)/shard_map/all_gather | solution.py:73
  570.2 9.2 %convolution_bitcast_fusion.5 = f32[2,16,128,1,1]{2,3,4,1,0:T(1,128)S(1)} fusion(f32[2,16,4,128,1]{3,4,2,1,0:T(1,128)S(1)} %bitcast.241, f32[2,16,4,128,128]{4,3,2,1,0:T(8,128)} %param.9), kind=kOutput, calls=%fused_computation.13 | convolution fusion | flops 25165824 | bytes 8470528 | tf_op jit(solution)/shard_map/srnij,srnj->sri/dot_general | solution.py:76
  587.0 52.6 %all-reduce.28.cloned.1.call-done = f32[128,2,128]{2,1,0:T(2,128)} async-done(((f32[128,2,128]{2,1,0:T(2,128)}), f32[128,2,128]{2,1,0:T(2,128)}) %all-reduce.28.cloned.1.call-update) | async-done | bytes 131088
  640.6 11.8 %psum.93 = f32[2,1]{0,1:T(1,128)S(1)} all-reduce(f32[2,1]{0,1:T(1,128)S(1)} %bitcast.262), channel_id=1, replica_groups=mesh['grp'=4,'sub'=8] {'sub'}, use_global_device_ids=true, to_apply=%region_25.26 | all-reduce | flops 2 | bytes 16 | tf_op jit(solution)/shard_map/psum | solution.py:116
  652.5 29.1 %all-gather.2 = f32[32,2,128]{2,1,0:T(2,128)S(1)} all-gather(f32[1,2,128]{2,1,0:T(2,128)S(1)} %fusion.48), channel_id=1, replica_groups=mesh['grp'=4,'sub'=8] {'grp','sub'}, dimensions={0}, use_global_device_ids=true | all-gather | bytes 33792 | tf_op jit(solution)/shard_map/all_gather | solution.py:125
  681.6 55.2 %scatter_custom_fusion.1 = f32[8193]{0:T(1024)S(1)} fusion(s32[8192]{0:T(1024)S(1)} %select_bitcast_fusion, f32[8192]{0:T(1024)S(1)} %bitcast.248, f32[]{:T(128)} %constant.41.clone.1), kind=kCustom, calls=%fused_computation.86 | custom fusion | flops 8192 | bytes 32776 | tf_op jit(solution)/shard_map/scatter-add | solution.py:126
  746.5 46.9 %all-reduce.10 = (f32[]{:T(128)}, f32[]{:T(128)}) all-reduce(f32[]{:T(128)} %get-tuple-element.3, f32[]{:T(128)} %get-tuple-element.2), channel_id=1, replica_groups=mesh['grp'=4,'sub'=8] {'grp','sub'}, use_global_device_ids=true, to_apply=%region_28.29 | all-reduce | flops 2 | bytes 16 | tf_op jit(solution)/shard_map/psum | solution.py:135
  (117 shorter events, 60.3 us)
Async XLA Ops:
  7.2 80.2 %all-reduce.20.cloned.1.call-start = ((), (), s32[]{:S(2)}) async-start(), calls=%async_computation.1 | async-start | bytes 262144
  19.4 10.2 %copy-start = (f32[2,16,4,128,128]{4,3,2,1,0:T(8,128)S(1)}, f32[2,16,4,128,128]{4,3,2,1,0:T(8,128)}, u32[]{:S(2)}) copy-start(f32[2,16,4,128,128]{4,3,2,1,0:T(8,128)} %param.9) | copy-start | bytes 25165828
  19.4 14.2 %copy-start.4 = (s32[2,16,4]{1,2,0:T(4,128)S(1)}, s32[2,16,4]{1,2,0:T(4,128)}, u32[]{:S(2)}) copy-start(s32[2,16,4]{1,2,0:T(4,128)} %param.10) | copy-start | bytes 1540
  19.4 15.4 %copy-start.10 = (s32[2,128]{1,0:T(2,128)S(1)}, s32[2,128]{1,0:T(2,128)}, u32[]{:S(2)}) copy-start(s32[2,128]{1,0:T(2,128)} %param.15) | copy-start | bytes 3076
  19.4 46.2 %copy-start.11 = (u32[32]{0:T(128)S(1)}, u32[32]{0:T(128)}, u32[]{:S(2)}) copy-start(u32[32]{0:T(128)} %constant.138) | copy-start | bytes 388
  19.4 67.9 %copy-start.2 = (f32[2,2048]{1,0:T(2,128)S(1)}, f32[2,2048]{1,0:T(2,128)}, u32[]{:S(2)}) copy-start(f32[2,2048]{1,0:T(2,128)} %param.12) | copy-start | bytes 49156
  19.4 67.9 %copy-start.6 = (f32[2,128]{1,0:T(2,128)S(1)}, f32[2,128]{1,0:T(2,128)}, u32[]{:S(2)}) copy-start(f32[2,128]{1,0:T(2,128)} %param.13) | copy-start | bytes 3076
  19.4 67.9 %copy-start.9 = (s32[2,1]{0,1:T(1,128)S(1)}, s32[2,1]{0,1:T(1,128)}, u32[]{:S(2)}) copy-start(s32[2,1]{0,1:T(1,128)} %param.11) | copy-start | bytes 28
  34.7 157.6 %all-reduce.22.cloned.1.call-start = ((), (), s32[]{:S(2)}) async-start(), calls=%async_computation.2 | async-start | bytes 262144
  122.8 166.7 %copy-start.5 = (f32[32,256]{1,0:T(8,128)S(1)}, f32[32,256]{1,0:T(8,128)}, u32[]{:S(2)}) copy-start(f32[32,256]{1,0:T(8,128)} %param.16) | copy-start | bytes 98308
  122.8 175.4 %copy-start.3 = (f32[32,256]{1,0:T(8,128)S(1)}, f32[32,256]{1,0:T(8,128)}, u32[]{:S(2)}) copy-start(f32[32,256]{1,0:T(8,128)} %param.17) | copy-start | bytes 98308
  139.5 259.9 %all-gather.5.cloned.1.call-start = ((), (), s32[]{:S(2)}) async-start(), calls=%async_computation | async-start | bytes 1081344 | tf_op jit(solution)/shard_map/all_gather | solution.py:99
  289.5 7.4 collective-permute-start.1
  291.7 6.4 collective-permute-start
  347.8 106.6 %all-reduce.24.cloned.1.call-start = ((), (), s32[]{:S(2)}) async-start(), calls=%async_computation.3 | async-start | bytes 262144
  357.9 96.5 %copy-start.7 = (f32[2,2048]{1,0:T(2,128)S(1)}, f32[2,2048]{1,0:T(2,128)}, u32[]{:S(2)}) copy-start(f32[2,2048]{1,0:T(2,128)} %param.14) | copy-start | bytes 49156
  374.6 160.4 %all-reduce.26.cloned.1.call-start = ((), (), s32[]{:S(2)}) async-start(), calls=%async_computation.4 | async-start | bytes 262144
  465.5 16.8 %copy-start.1 = (f32[32,256]{1,0:T(8,128)S(1)}, f32[32,256]{1,0:T(8,128)}, u32[]{:S(2)}) copy-start(f32[32,256]{1,0:T(8,128)} %broadcast_multiply_fusion) | copy-start | bytes 98308
  482.2 157.4 %all-reduce.28.cloned.1.call-start = ((), (), s32[]{:S(2)}) async-start(), calls=%async_computation.5 | async-start | bytes 262144
  482.3 104.6 %collective-permute-start.3 = (f32[1,256]{1,0:T(1,128)S(1)}, f32[1,256]{1,0:T(1,128)S(1)}, u32[]{:S(2)}, u32[]{:S(2)}) collective-permute-start(f32[1,256]{1,0:T(1,128)S(1)} %get-tuple-element.22), channel_id=1, source_target_pairs={{0,1},{1,2},{2,3},{3,4},{4,5},{5,6},{6,7},{7,8},{8,9},{9,10},{10,1... | collective-permute-start | bytes 3080 | tf_op jit(solution)/shard_map/ppermute | solution.py:19
  484.5 102.4 %collective-permute-start.2 = (f32[1,256]{1,0:T(1,128)S(1)}, f32[1,256]{1,0:T(1,128)S(1)}, u32[]{:S(2)}, u32[]{:S(2)}) collective-permute-start(f32[1,256]{1,0:T(1,128)S(1)} %get-tuple-element.23), channel_id=1, source_target_pairs={{1,0},{2,1},{3,2},{4,3},{5,4},{6,5},{7,6},{8,7},{9,8},{10,9},{11,1... | collective-permute-start | bytes 3080 | tf_op jit(solution)/shard_map/ppermute | solution.py:20
  652.5 142.8 %copy-start.8 = (f32[2,2048]{1,0:T(2,128)}, f32[2,2048]{1,0:T(2,128)S(1)}, u32[]{:S(2)}) copy-start(f32[2,2048]{1,0:T(2,128)S(1)} %multiply_add_fusion.1) | copy-start | bytes 49156
  737.0 7.4 collective-permute-start.5
  739.2 6.4 collective-permute-start.4
Sparse Core Ops, SparseCore 0:
  34.8 52.4 all-reduce.19
  139.6 52.5 all-reduce.21
  347.9 51.4 all-gather.4
  402.3 51.9 all-reduce.23
  482.3 52.5 all-reduce.25
  587.0 52.5 all-reduce.27
where the time goes:
time: 811 us; the launch traced here: 802 us
  blocking collectives  299 us (37%)
  waiting for transfers between devices  251 us (31%)
  other arithmetic  120 us (15%)
  matrix products  78.1 us (10%)
  starting transfers between devices  21.4 us (3%)
  between operations  18.1 us (2%)
  local copies, waits for them, and re-layouts  14.3 us (2%)
    unnamed x11, waiting for transfers between devices  224 us
    scatter-add x2, other arithmetic, body(): jax.ops.segment_sum(lam_all.reshape(-1), seg_idx.reshape(-1), num_segment...  110 us
    psum x2, blocking collectives, body(): lax.psum((jnp.sum(resid_g * resid_g), jnp.sum(resid_g * image_g)), ('grp'...  93.8 us
    all_gather x2, blocking collectives, body(): lam_all = lax.all_gather(lam, ('grp', 'sub'), axis=0, tiled=True)  58.2 us
    psum x4, blocking collectives, norm_sum(): return lax.psum(row_sum(vector, vector), 'sub')  47.2 us
    dot_general x5, matrix products, sub_apply(): strain = jnp.einsum('srnij,srnj->sri', stiff_blocks, picked, precision=HIGH)  46.9 us
    all_gather x5, blocking collectives, sub_apply(): whole = lax.all_gather(vector, 'sub', axis=1, tiled=True)  45.5 us
    all_gather x1, blocking collectives, body(): all_map = lax.all_gather(iface_map, ('grp', 'sub'), axis=0, tiled=True)  30.8 us
  transfers between devices with their start and end apart: 12, of which 8 were waited for; matrix products, arithmetic and copies ran while one was open for 5% of the time, Pallas kernels for 0%

commit v1 on v0

--- a/solution.py
+++ b/solution.py
@@ -107,7 +107,7 @@
             resid = rhs - sub_apply(field)
 
         def norm_sum(vector):
-            return lax.psum(row_sum(vector, vector), "sub")
+            return jnp.sum(lax.all_gather(row_sum(vector, vector), "sub"), axis=0)
 
         direction = resid
         norm_now = norm_sum(resid)

time: 811 us -> 815 us (level)
    psum x4 -> x0, blocking collectives: 47.2 us -> none  [norm_sum(): return lax.psum(row_sum(vector, vector), 'sub')]
    unnamed x0 -> x2, blocking collectives: none -> 24.1 us
    psum x2 -> x4, blocking collectives: 23.6 us -> 47.2 us  [body(): alpha = norm_now / lax.psum(row_sum(direction, image), 'sub')]
where the time goes in v1:
time: 815 us; the launch traced here: 806 us
  blocking collectives  300 us (37%)
  waiting for transfers between devices  254 us (31%)
  other arithmetic  121 us (15%)
  matrix products  78.1 us (10%)
  starting transfers between devices  19.1 us (2%)
  between operations  18.7 us (2%)
  local copies, waits for them, and re-layouts  15.6 us (2%)
    unnamed x11, waiting for transfers between devices  227 us
    scatter-add x2, other arithmetic, body(): jax.ops.segment_sum(lam_all.reshape(-1), seg_idx.reshape(-1), num_segment...  110 us
    psum x2, blocking collectives, body(): lax.psum((jnp.sum(resid_g * resid_g), jnp.sum(resid_g * image_g)), ('grp'...  93.8 us
    all_gather x2, blocking collectives, body(): lam_all = lax.all_gather(lam, ('grp', 'sub'), axis=0, tiled=True)  58.2 us
    psum x4, blocking collectives, body(): alpha = norm_now / lax.psum(row_sum(direction, image), 'sub')  47.2 us
    dot_general x5, matrix products, sub_apply(): strain = jnp.einsum('srnij,srnj->sri', stiff_blocks, picked, precision=HIGH)  46.9 us
    all_gather x5, blocking collectives, sub_apply(): whole = lax.all_gather(vector, 'sub', axis=1, tiled=True)  45.5 us
    all_gather x1, blocking collectives, body(): all_map = lax.all_gather(iface_map, ('grp', 'sub'), axis=0, tiled=True)  30.8 us
  transfers between devices with their start and end apart: 12, of which 8 were waited for; matrix products, arithmetic and copies ran while one was open for 5% of the time, Pallas kernels for 0%

profile of v1, /device:TPU:12, one launch (start us, length us, event | category | flops | bytes accessed | tf_op | source)
XLA Modules:
  0.0 806.2 jit_solution(9866449710576111617)
XLA Ops:
  8.9 9.2 %all_gather.41 = f32[2,16384]{1,0:T(2,128)S(1)} all-gather(f32[2,2048]{1,0:T(2,128)S(1)} %compare_select_fusion.6), channel_id=1, replica_groups=mesh['grp'=4,'sub'=8] {'sub'}, dimensions={1}, use_global_device_ids=true | all-gather | bytes 147456 | tf_op jit(solution)/shard_map/all_gather | solution.py:73
  19.4 10.1 %convolution_bitcast_fusion.9 = f32[2,16,128,1,1]{2,3,4,1,0:T(1,128)S(1)} fusion(f32[2,16,4,128,1]{3,4,2,1,0:T(1,128)S(1)} %bitcast.251, f32[2,16,4,128,128]{4,3,2,1,0:T(8,128)} %param.9), kind=kOutput, calls=%fused_computation.17 | convolution fusion | flops 25165824 | bytes 8470528 | tf_op jit(solution)/shard_map/srnij,srnj->sri/dot_general | solution.py:76
  34.8 30.8 %all-gather.4 = s32[32,2,128]{2,1,0:T(2,128)S(1)} all-gather(s32[1,2,128]{2,1,0:T(2,128)S(1)} %bitcast.266), channel_id=1, replica_groups=mesh['grp'=4,'sub'=8] {'grp','sub'}, dimensions={0}, use_global_device_ids=true | all-gather | bytes 33792 | tf_op jit(solution)/shard_map/all_gather | solution.py:89
  67.5 19.9 %all-reduce.24.cloned.1.call-done = f32[128,2,128]{2,1,0:T(2,128)} async-done(((f32[128,2,128]{2,1,0:T(2,128)}), f32[128,2,128]{2,1,0:T(2,128)}) %all-reduce.24.cloned.1.call-update) | async-done | bytes 131088
  88.5 11.8 %all-reduce.17 = (f32[2,1]{0,1:T(1,128)S(1)}, f32[16]{0:T(128)S(1)}) all-reduce(f32[2,1]{0,1:T(1,128)S(1)} %bitcast.267, f32[16]{0:T(128)S(1)} %dynamic-update-slice), channel_id=1, replica_groups=mesh['grp'=4,'sub'=8] {'sub'}, use_global_device_ids=true, to_apply=%region_4.5 | all-reduce | flops 18 | bytes 144 | tf_op jit(solution)/shard_map/psum | solution.py:116
  100.9 11.8 %all-reduce.6 = f32[16]{0:T(128)S(1)} all-reduce(f32[16]{0:T(128)S(1)} %dynamic-update-slice.1), channel_id=3, replica_groups=mesh['grp'=4,'sub'=8] {'sub'}, use_global_device_ids=true, to_apply=%add.6 | all-reduce | flops 16 | bytes 128
  112.9 9.3 %all_gather.43 = f32[2,16384]{1,0:T(2,128)S(1)} all-gather(f32[2,2048]{1,0:T(2,128)S(1)} %multiply_add_fusion.4), channel_id=1, replica_groups=mesh['grp'=4,'sub'=8] {'sub'}, dimensions={1}, use_global_device_ids=true | all-gather | bytes 147456 | tf_op jit(solution)/shard_map/all_gather | solution.py:73
  123.5 9.2 %convolution_bitcast_fusion.8 = f32[2,16,128,1,1]{2,3,4,1,0:T(1,128)S(1)} fusion(f32[2,16,4,128,1]{3,4,2,1,0:T(1,128)S(1)} %bitcast.252, f32[2,16,4,128,128]{4,3,2,1,0:T(8,128)} %param.9), kind=kOutput, calls=%fused_computation.16 | convolution fusion | flops 25165824 | bytes 8470528 | tf_op jit(solution)/shard_map/srnij,srnj->sri/dot_general | solution.py:76
  132.7 6.4 fusion.59
  140.2 52.7 %all-reduce.26.cloned.1.call-done = f32[128,2,128]{2,1,0:T(2,128)} async-done(((f32[128,2,128]{2,1,0:T(2,128)}), f32[128,2,128]{2,1,0:T(2,128)}) %all-reduce.26.cloned.1.call-update) | async-done | bytes 131088
  193.8 11.8 %psum.57 = f32[2,1]{0,1:T(1,128)S(1)} all-reduce(f32[2,1]{0,1:T(1,128)S(1)} %bitcast.270), channel_id=1, replica_groups=mesh['grp'=4,'sub'=8] {'sub'}, use_global_device_ids=true, to_apply=%region_9.10 | all-reduce | flops 2 | bytes 16 | tf_op jit(solution)/shard_map/psum | solution.py:116
  205.7 29.1 %all-gather.5 = f32[32,2,128]{2,1,0:T(2,128)S(1)} all-gather(f32[1,2,128]{2,1,0:T(2,128)S(1)} %fusion.49), channel_id=1, replica_groups=mesh['grp'=4,'sub'=8] {'grp','sub'}, dimensions={0}, use_global_device_ids=true | all-gather | bytes 33792 | tf_op jit(solution)/shard_map/all_gather | solution.py:125
  234.8 55.2 %scatter_custom_fusion = f32[8193]{0:T(1024)S(1)} fusion(s32[8192]{0:T(1024)S(1)} %select_bitcast_fusion, f32[8192]{0:T(1024)S(1)} %bitcast.258, f32[]{:T(128)} %constant.41.clone.1), kind=kCustom, calls=%fused_computation.88 | custom fusion | flops 8192 | bytes 32776 | tf_op jit(solution)/shard_map/scatter-add | solution.py:126
  299.7 46.9 %all-reduce.15 = (f32[]{:T(128)}, f32[]{:T(128)}) all-reduce(f32[]{:T(128)} %get-tuple-element.5, f32[]{:T(128)} %get-tuple-element.4), channel_id=1, replica_groups=mesh['grp'=4,'sub'=8] {'grp','sub'}, use_global_device_ids=true, to_apply=%region_12.13 | all-reduce | flops 2 | bytes 16 | tf_op jit(solution)/shard_map/psum | solution.py:135
  348.5 8.8 %all_gather.46 = f32[2,16384]{1,0:T(2,128)S(1)} all-gather(f32[2,2048]{1,0:T(2,128)S(1)} %multiply_add_fusion.3), channel_id=1, replica_groups=mesh['grp'=4,'sub'=8] {'sub'}, dimensions={1}, use_global_device_ids=true | all-gather | bytes 147456 | tf_op jit(solution)/shard_map/all_gather | solution.py:73
  358.6 9.2 %convolution_bitcast_fusion.7 = f32[2,16,128,1,1]{2,3,4,1,0:T(1,128)S(1)} fusion(f32[2,16,4,128,1]{3,4,2,1,0:T(1,128)S(1)} %bitcast.253, f32[2,16,4,128,128]{4,3,2,1,0:T(8,128)} %param.9), kind=kOutput, calls=%fused_computation.15 | convolution fusion | flops 25165824 | bytes 8470528 | tf_op jit(solution)/shard_map/srnij,srnj->sri/dot_general | solution.py:76
  367.8 6.4 fusion.60
  375.3 24.8 %all-gather.9.cloned.1.call-done = f32[1024,256]{1,0:T(8,128)} async-done(((f32[32,256]{1,0:T(8,128)}), f32[1024,256]{1,0:T(8,128)}) %all-gather.9.cloned.1.call-update) | async-done | bytes 1048592 | tf_op jit(solution)/shard_map/all_gather | solution.py:99
  403.6 51.4 %all-reduce.28.cloned.1.call-done = f32[128,2,128]{2,1,0:T(2,128)} async-done(((f32[128,2,128]{2,1,0:T(2,128)}), f32[128,2,128]{2,1,0:T(2,128)}) %all-reduce.28.cloned.1.call-update) | async-done | bytes 131088
  455.8 9.1 %all_gather.48 = f32[2,16384]{1,0:T(2,128)S(1)} all-gather(f32[2,2048]{1,0:T(2,128)S(1)} %fusion.35), channel_id=1, replica_groups=mesh['grp'=4,'sub'=8] {'sub'}, dimensions={1}, use_global_device_ids=true | all-gather | bytes 147456 | tf_op jit(solution)/shard_map/all_gather | solution.py:73
  466.2 9.2 %convolution_bitcast_fusion.6 = f32[2,16,128,1,1]{2,3,4,1,0:T(1,128)S(1)} fusion(f32[2,16,4,128,1]{3,4,2,1,0:T(1,128)S(1)} %bitcast.254, f32[2,16,4,128,128]{4,3,2,1,0:T(8,128)} %param.9), kind=kOutput, calls=%fused_computation.14 | convolution fusion | flops 25165824 | bytes 8470528 | tf_op jit(solution)/shard_map/srnij,srnj->sri/dot_general | solution.py:76
  475.4 6.4 fusion.61
  485.2 50.4 %all-reduce.30.cloned.1.call-done = f32[128,2,128]{2,1,0:T(2,128)} async-done(((f32[128,2,128]{2,1,0:T(2,128)}), f32[128,2,128]{2,1,0:T(2,128)}) %all-reduce.30.cloned.1.call-update) | async-done | bytes 131088
  536.8 11.8 %all-reduce.16 = (f32[2,1]{0,1:T(1,128)S(1)}, f32[16]{0:T(128)S(1)}) all-reduce(f32[2,1]{0,1:T(1,128)S(1)} %bitcast.268, f32[16]{0:T(128)S(1)} %dynamic-update-slice.2), channel_id=1, replica_groups=mesh['grp'=4,'sub'=8] {'sub'}, use_global_device_ids=true, to_apply=%region_20.21 | all-reduce | flops 18 | bytes 144 | tf_op jit(solution)/shard_map/psum | solution.py:116
  551.1 12.3 %all-reduce.8 = f32[16]{0:T(128)S(1)} all-reduce(f32[16]{0:T(128)S(1)} %dynamic-update-slice.3), channel_id=5, replica_groups=mesh['grp'=4,'sub'=8] {'sub'}, use_global_device_ids=true, to_apply=%add.8 | all-reduce | flops 16 | bytes 128
  563.6 9.1 %all_gather.50 = f32[2,16384]{1,0:T(2,128)S(1)} all-gather(f32[2,2048]{1,0:T(2,128)S(1)} %multiply_add_fusion.2), channel_id=1, replica_groups=mesh['grp'=4,'sub'=8] {'sub'}, dimensions={1}, use_global_device_ids=true | all-gather | bytes 147456 | tf_op jit(solution)/shard_map/all_gather | solution.py:73
  574.0 9.2 %convolution_bitcast_fusion.5 = f32[2,16,128,1,1]{2,3,4,1,0:T(1,128)S(1)} fusion(f32[2,16,4,128,1]{3,4,2,1,0:T(1,128)S(1)} %bitcast.250, f32[2,16,4,128,128]{4,3,2,1,0:T(8,128)} %param.9), kind=kOutput, calls=%fused_computation.13 | convolution fusion | flops 25165824 | bytes 8470528 | tf_op jit(solution)/shard_map/srnij,srnj->sri/dot_general | solution.py:76
  590.8 52.6 %all-reduce.32.cloned.1.call-done = f32[128,2,128]{2,1,0:T(2,128)} async-done(((f32[128,2,128]{2,1,0:T(2,128)}), f32[128,2,128]{2,1,0:T(2,128)}) %all-reduce.32.cloned.1.call-update) | async-done | bytes 131088
  644.4 11.8 %psum.61 = f32[2,1]{0,1:T(1,128)S(1)} all-reduce(f32[2,1]{0,1:T(1,128)S(1)} %bitcast.269), channel_id=1, replica_groups=mesh['grp'=4,'sub'=8] {'sub'}, use_global_device_ids=true, to_apply=%region_25.26 | all-reduce | flops 2 | bytes 16 | tf_op jit(solution)/shard_map/psum | solution.py:116
  656.3 29.1 %all-gather.6 = f32[32,2,128]{2,1,0:T(2,128)S(1)} all-gather(f32[1,2,128]{2,1,0:T(2,128)S(1)} %fusion.48), channel_id=1, replica_groups=mesh['grp'=4,'sub'=8] {'grp','sub'}, dimensions={0}, use_global_device_ids=true | all-gather | bytes 33792 | tf_op jit(solution)/shard_map/all_gather | solution.py:125
  685.4 55.2 %scatter_custom_fusion.1 = f32[8193]{0:T(1024)S(1)} fusion(s32[8192]{0:T(1024)S(1)} %select_bitcast_fusion, f32[8192]{0:T(1024)S(1)} %bitcast.257, f32[]{:T(128)} %constant.41.clone.1), kind=kCustom, calls=%fused_computation.86 | custom fusion | flops 8192 | bytes 32776 | tf_op jit(solution)/shard_map/scatter-add | solution.py:126
  750.3 46.9 %all-reduce.14 = (f32[]{:T(128)}, f32[]{:T(128)}) all-reduce(f32[]{:T(128)} %get-tuple-element.3, f32[]{:T(128)} %get-tuple-element.2), channel_id=1, replica_groups=mesh['grp'=4,'sub'=8] {'grp','sub'}, use_global_device_ids=true, to_apply=%region_28.29 | all-reduce | flops 2 | bytes 16 | tf_op jit(solution)/shard_map/psum | solution.py:135
  (133 shorter events, 59.5 us)
Async XLA Ops:
  7.2 80.2 %all-reduce.24.cloned.1.call-start = ((), (), s32[]{:S(2)}) async-start(), calls=%async_computation.1 | async-start | bytes 262144
  19.4 10.2 %copy-start = (f32[2,16,4,128,128]{4,3,2,1,0:T(8,128)S(1)}, f32[2,16,4,128,128]{4,3,2,1,0:T(8,128)}, u32[]{:S(2)}) copy-start(f32[2,16,4,128,128]{4,3,2,1,0:T(8,128)} %param.9) | copy-start | bytes 25165828
  19.4 14.2 %copy-start.4 = (s32[2,16,4]{1,2,0:T(4,128)S(1)}, s32[2,16,4]{1,2,0:T(4,128)}, u32[]{:S(2)}) copy-start(s32[2,16,4]{1,2,0:T(4,128)} %param.10) | copy-start | bytes 1540
  19.4 15.4 %copy-start.10 = (s32[2,128]{1,0:T(2,128)S(1)}, s32[2,128]{1,0:T(2,128)}, u32[]{:S(2)}) copy-start(s32[2,128]{1,0:T(2,128)} %param.15) | copy-start | bytes 3076
  19.4 46.2 %copy-start.11 = (u32[32]{0:T(128)S(1)}, u32[32]{0:T(128)}, u32[]{:S(2)}) copy-start(u32[32]{0:T(128)} %constant.138) | copy-start | bytes 388
  19.4 67.9 %copy-start.2 = (f32[2,2048]{1,0:T(2,128)S(1)}, f32[2,2048]{1,0:T(2,128)}, u32[]{:S(2)}) copy-start(f32[2,2048]{1,0:T(2,128)} %param.12) | copy-start | bytes 49156
  19.4 67.9 %copy-start.6 = (f32[2,128]{1,0:T(2,128)S(1)}, f32[2,128]{1,0:T(2,128)}, u32[]{:S(2)}) copy-start(f32[2,128]{1,0:T(2,128)} %param.13) | copy-start | bytes 3076
  19.4 67.9 %copy-start.9 = (s32[2,1]{0,1:T(1,128)S(1)}, s32[2,1]{0,1:T(1,128)}, u32[]{:S(2)}) copy-start(s32[2,1]{0,1:T(1,128)} %param.11) | copy-start | bytes 28
  34.7 158.2 %all-reduce.26.cloned.1.call-start = ((), (), s32[]{:S(2)}) async-start(), calls=%async_computation.2 | async-start | bytes 262144
  123.5 166.7 %copy-start.5 = (f32[32,256]{1,0:T(8,128)S(1)}, f32[32,256]{1,0:T(8,128)}, u32[]{:S(2)}) copy-start(f32[32,256]{1,0:T(8,128)} %param.16) | copy-start | bytes 98308
  123.5 175.4 %copy-start.3 = (f32[32,256]{1,0:T(8,128)S(1)}, f32[32,256]{1,0:T(8,128)}, u32[]{:S(2)}) copy-start(f32[32,256]{1,0:T(8,128)} %param.17) | copy-start | bytes 98308
  140.2 259.9 %all-gather.9.cloned.1.call-start = ((), (), s32[]{:S(2)}) async-start(), calls=%async_computation | async-start | bytes 1081344 | tf_op jit(solution)/shard_map/all_gather | solution.py:99
  290.1 7.4 collective-permute-start.1
  292.4 6.4 collective-permute-start
  348.5 106.6 %all-reduce.28.cloned.1.call-start = ((), (), s32[]{:S(2)}) async-start(), calls=%async_computation.3 | async-start | bytes 262144
  358.5 96.5 %copy-start.7 = (f32[2,2048]{1,0:T(2,128)S(1)}, f32[2,2048]{1,0:T(2,128)}, u32[]{:S(2)}) copy-start(f32[2,2048]{1,0:T(2,128)} %param.14) | copy-start | bytes 49156
  375.2 160.4 %all-reduce.30.cloned.1.call-start = ((), (), s32[]{:S(2)}) async-start(), calls=%async_computation.4 | async-start | bytes 262144
  466.2 16.8 %copy-start.1 = (f32[32,256]{1,0:T(8,128)S(1)}, f32[32,256]{1,0:T(8,128)}, u32[]{:S(2)}) copy-start(f32[32,256]{1,0:T(8,128)} %broadcast_multiply_fusion) | copy-start | bytes 98308
  482.9 160.5 %all-reduce.32.cloned.1.call-start = ((), (), s32[]{:S(2)}) async-start(), calls=%async_computation.5 | async-start | bytes 262144
  483.0 107.7 %collective-permute-start.3 = (f32[1,256]{1,0:T(1,128)S(1)}, f32[1,256]{1,0:T(1,128)S(1)}, u32[]{:S(2)}, u32[]{:S(2)}) collective-permute-start(f32[1,256]{1,0:T(1,128)S(1)} %get-tuple-element.22), channel_id=1, source_target_pairs={{0,1},{1,2},{2,3},{3,4},{4,5},{5,6},{6,7},{7,8},{8,9},{9,10},{10,1... | collective-permute-start | bytes 3080 | tf_op jit(solution)/shard_map/ppermute | solution.py:19
  549.2 41.5 %collective-permute-start.2 = (f32[1,256]{1,0:T(1,128)S(1)}, f32[1,256]{1,0:T(1,128)S(1)}, u32[]{:S(2)}, u32[]{:S(2)}) collective-permute-start(f32[1,256]{1,0:T(1,128)S(1)} %get-tuple-element.23), channel_id=1, source_target_pairs={{1,0},{2,1},{3,2},{4,3},{5,4},{6,5},{7,6},{8,7},{9,8},{10,9},{11,1... | collective-permute-start | bytes 3080 | tf_op jit(solution)/shard_map/ppermute | solution.py:20
  656.3 142.8 %copy-start.8 = (f32[2,2048]{1,0:T(2,128)}, f32[2,2048]{1,0:T(2,128)S(1)}, u32[]{:S(2)}) copy-start(f32[2,2048]{1,0:T(2,128)S(1)} %multiply_add_fusion.1) | copy-start | bytes 49156
  740.8 7.4 collective-permute-start.5
  743.0 6.4 collective-permute-start.4
Sparse Core Ops, SparseCore 0:
  34.8 52.4 all-reduce.23
  140.3 52.5 all-reduce.25
  348.6 51.4 all-gather.8
  403.0 51.9 all-reduce.27
  483.0 52.5 all-reduce.29
  590.8 52.5 all-reduce.31
